TPU v7x, 32 devices: a whole 2x2x4 slice. The times are simulated.
32 devices in a mesh: dp: 8 (over z, y), mp: 4 (over x, core).
Axes of the slice: x: 2, y: 2, z: 4, core: 2. Of those that a mesh axis runs over, the one named last changes fastest.
Arguments:
- tokens: bfloat16 [16384, 1024], P(('dp', 'mp')), may hold values from -6 to 6
- segment_ids: int32 [16384], P(('dp', 'mp')), may hold values from 0 to 63, never falling along the last dimension, each value on 1 to 512 neighbouring positions
- w_qkv: bfloat16 [3, 1024, 1024], P(None, None, 'mp'), may hold values from -0.1875 to 0.1875
- b_qv: bfloat16 [2, 1024], P(None, 'mp'), may hold values from -1.75 to 1.75
- w_out: bfloat16 [1024, 1024], P('mp'), may hold values from -2 to 2
- b_out: bfloat16 [1024], replicated, may hold values from -1.75 to 1.75
- w_up: bfloat16 [1024, 4096], P(None, 'mp'), may hold values from -0.1875 to 0.1875
- b_up: bfloat16 [4096], P('mp'), may hold values from -1.75 to 1.75
- w_down: bfloat16 [4096, 1024], P('mp'), may hold values from -0.125 to 0.125
- b_down: bfloat16 [1024], replicated, may hold values from -1.75 to 1.75
- ln_gain: float32 [2, 1024], replicated, may hold values from 0.5 to 1.5
- ln_bias: float32 [2, 1024], replicated, may hold values from -1.75 to 1.75
- out_grad: bfloat16 [16384, 1024], P(('dp', 'mp')), may hold values from -6 to 6
Outputs:
- block_out: bfloat16 [16384, 1024], P(('dp', 'mp'))
- grad_in: float32 [16384, 1024], P(('dp', 'mp'))
- grad_qkv: float32 [3, 1024, 1024], P(None, None, 'mp')
- grad_bqv: float32 [2, 1024], P(None, 'mp')
- grad_wout: float32 [1024, 1024], P('mp')
- grad_bout: float32 [1024], replicated
- grad_up: float32 [1024, 4096], P(None, 'mp')
- grad_bup: float32 [4096], P('mp')
- grad_down: float32 [4096, 1024], P('mp')
- grad_bdown: float32 [1024], replicated
- grad_gain: float32 [2, 1024], replicated
- grad_shift: float32 [2, 1024], replicated
Inputs may be any that keep to these rules, and one draw needn't show every extreme that they name: `segment_ids`: along all frames in order, segment numbers never fall; each segment covers 1 to 512 frames and one covers exactly 512; attention never crosses a row of 1024 frames.
All inputs are finite; a program needn't handle non-finite values.
Results may differ from a plain program's by a relative error of at most 0.02.
Values may be sent and summed in bfloat16 or wider, within the bound.
No kernel may reach another device: no remote copies, remote signals or barrier semaphores. Data moves between devices by JAX's collectives and lax.ppermute only.
A program may use at most 192 MiB of HBM per device.

v0:
```python
import jax
import jax.numpy as jnp
from jax import lax
from jax.sharding import PartitionSpec as P

HD = 64
LEN = 1024
QBLK = 512
EPS = 1e-05


def norm_rows(values, gain, shift):
    center = values - jnp.mean(values, axis=-1, keepdims=True)
    spread = jnp.mean(center * center, axis=-1, keepdims=True)
    return center * lax.rsqrt(spread + EPS) * gain + shift


def split_heads(flat, rows):
    return flat.reshape(rows, LEN, flat.shape[1] // HD, HD)


def block_scores(query, keys, seg_q, seg_k, offset):
    scores = jnp.einsum(
        "rqhd,rkhd->rhqk", query, keys, preferred_element_type=jnp.float32
    ) * HD ** (-0.5)
    q_pos = offset + jnp.arange(query.shape[1], dtype=jnp.int32)
    k_pos = jnp.arange(keys.shape[1], dtype=jnp.int32)
    allowed = (seg_q[:, :, None] == seg_k[:, None, :]) & (
        k_pos[None, None, :] <= q_pos[None, :, None]
    )
    return jnp.where(allowed[:, None], scores, -1e30)


def attention_forward(query, keys, values, seg_all):
    rows = query.shape[0] // LEN
    q4 = split_heads(query, rows)
    k4 = split_heads(keys, rows)
    v4 = split_heads(values, rows)
    seg2 = seg_all.reshape(rows, LEN)
    outputs = []
    totals = []
    for block in range(LEN // QBLK):
        first = block * QBLK
        end = first + QBLK
        scores = block_scores(
            q4[:, first:end], k4[:, :end], seg2[:, first:end], seg2[:, :end], first
        )
        top = jnp.max(scores, axis=-1, keepdims=True)
        expd = jnp.exp(scores - top)
        summed = jnp.sum(expd, axis=-1, keepdims=True)
        weights = (expd / summed).astype(jnp.bfloat16)
        outputs.append(
            jnp.einsum("rhqk,rkhd->rqhd", weights, v4[:, :end], preferred_element_type=jnp.float32)
        )
        totals.append(top + jnp.log(summed))
    attended = jnp.concatenate(outputs, axis=1).reshape(query.shape).astype(jnp.bfloat16)
    return (attended, totals)


def attention_backward(query, keys, values, seg_all, totals, grad_att):
    rows = query.shape[0] // LEN
    q4 = split_heads(query, rows)
    k4 = split_heads(keys, rows)
    v4 = split_heads(values, rows)
    g4 = split_heads(grad_att, rows)
    seg2 = seg_all.reshape(rows, LEN)
    scale = HD ** (-0.5)
    grad_k = jnp.zeros(k4.shape, jnp.float32)
    grad_v = jnp.zeros(v4.shape, jnp.float32)
    grad_q_parts = []
    for block in range(LEN // QBLK):
        first = block * QBLK
        end = first + QBLK
        scores = block_scores(
            q4[:, first:end], k4[:, :end], seg2[:, first:end], seg2[:, :end], first
        )
        probs = jnp.exp(scores - totals[block])
        weights = probs.astype(jnp.bfloat16)
        grad_w = jnp.einsum(
            "rqhd,rkhd->rhqk", g4[:, first:end], v4[:, :end], preferred_element_type=jnp.float32
        )
        delta = jnp.sum(probs * grad_w, axis=-1, keepdims=True)
        grad_s = (probs * (grad_w - delta)).astype(jnp.bfloat16)
        grad_q_parts.append(
            jnp.einsum("rhqk,rkhd->rqhd", grad_s, k4[:, :end], preferred_element_type=jnp.float32)
            * scale
        )
        padding = ((0, 0), (0, LEN - end), (0, 0), (0, 0))
        grad_k = grad_k + jnp.pad(
            jnp.einsum(
                "rhqk,rqhd->rkhd", grad_s, q4[:, first:end], preferred_element_type=jnp.float32
            )
            * scale,
            padding,
        )
        grad_v = grad_v + jnp.pad(
            jnp.einsum(
                "rhqk,rqhd->rkhd", weights, g4[:, first:end], preferred_element_type=jnp.float32
            ),
            padding,
        )
    shape = query.shape
    grad_q = jnp.concatenate(grad_q_parts, axis=1).reshape(shape).astype(jnp.bfloat16)
    return (
        grad_q,
        grad_k.reshape(shape).astype(jnp.bfloat16),
        grad_v.reshape(shape).astype(jnp.bfloat16),
    )


def shards(
    tokens,
    segment_ids,
    w_qkv,
    b_qv,
    w_out,
    b_out,
    w_up,
    b_up,
    w_down,
    b_down,
    ln_gain,
    ln_bias,
    out_grad,
):
    resid = tokens.astype(jnp.float32)
    qv_bias = b_qv.astype(jnp.float32)
    up_bias = b_up.astype(jnp.float32)
    local_rows = tokens.shape[0]
    normed, first_back = jax.vjp(norm_rows, resid, ln_gain[0], ln_bias[0])
    lowered = normed.astype(jnp.bfloat16)
    joined, seg_all = (
        lax.all_gather(lowered, "mp", axis=0, tiled=True),
        lax.all_gather(segment_ids, "mp", axis=0, tiled=True),
    )
    query = (jnp.dot(joined, w_qkv[0], preferred_element_type=jnp.float32) + qv_bias[0]).astype(
        jnp.bfloat16
    )
    keys = jnp.dot(joined, w_qkv[1], preferred_element_type=jnp.float32).astype(jnp.bfloat16)
    values = (jnp.dot(joined, w_qkv[2], preferred_element_type=jnp.float32) + qv_bias[1]).astype(
        jnp.bfloat16
    )
    query, keys, values = (query, keys, values)
    attended, totals = attention_forward(query, keys, values, seg_all)
    attn_sum = lax.psum_scatter(
        jnp.dot(attended, w_out, preferred_element_type=jnp.float32).astype(jnp.bfloat16),
        "mp",
        scatter_dimension=0,
        tiled=True,
    ).astype(jnp.float32)
    mixed = resid + attn_sum + b_out.astype(jnp.float32)
    normed2, second_back = jax.vjp(norm_rows, mixed, ln_gain[1], ln_bias[1])
    lowered2 = normed2.astype(jnp.bfloat16)
    joined2 = lax.all_gather(lowered2, "mp", axis=0, tiled=True)
    pre_act = jnp.dot(joined2, w_up, preferred_element_type=jnp.float32) + up_bias
    pre_act, activ = (pre_act, jax.nn.gelu(pre_act, approximate=False).astype(jnp.bfloat16))
    block_out = (
        mixed
        + lax.psum_scatter(
            jnp.dot(activ, w_down, preferred_element_type=jnp.float32).astype(jnp.bfloat16),
            "mp",
            scatter_dimension=0,
            tiled=True,
        ).astype(jnp.float32)
        + b_down.astype(jnp.float32)
    ).astype(jnp.bfloat16)
    grad_y = out_grad.astype(jnp.float32)
    grad_z = lax.all_gather(out_grad, "mp", axis=0, tiled=True)
    grad_down = jnp.einsum("tf,td->fd", activ, grad_z, preferred_element_type=jnp.float32)
    grad_bdown = jnp.sum(grad_z, axis=0, dtype=jnp.float32)
    grad_act = jnp.einsum("td,fd->tf", grad_z, w_down, preferred_element_type=jnp.float32)
    gelu_back = jax.vjp(lambda value: jax.nn.gelu(value, approximate=False), pre_act)[1]
    grad_pre = gelu_back(grad_act)[0].astype(jnp.bfloat16)
    grad_up = jnp.einsum("td,tf->df", joined2, grad_pre, preferred_element_type=jnp.float32)
    grad_bup = jnp.sum(grad_pre, axis=0, dtype=jnp.float32)
    grad_n2 = lax.psum_scatter(
        jnp.einsum("tf,df->td", grad_pre, w_up, preferred_element_type=jnp.float32).astype(
            jnp.bfloat16
        ),
        "mp",
        scatter_dimension=0,
        tiled=True,
    ).astype(jnp.float32)
    grad_h, grad_g2, grad_s2 = second_back(grad_n2)
    grad_h = grad_h + grad_y
    grad_branch = lax.all_gather(grad_h.astype(jnp.bfloat16), "mp", axis=0, tiled=True)
    grad_wout = jnp.einsum("tc,td->cd", attended, grad_branch, preferred_element_type=jnp.float32)
    grad_bout = jnp.sum(grad_branch, axis=0, dtype=jnp.float32)
    grad_att = jnp.einsum(
        "td,cd->tc", grad_branch, w_out, preferred_element_type=jnp.float32
    ).astype(jnp.bfloat16)
    grad_q, grad_k, grad_v = attention_backward(query, keys, values, seg_all, totals, grad_att)
    grad_qkv = jnp.stack(
        [
            jnp.einsum("td,tc->dc", joined, piece, preferred_element_type=jnp.float32)
            for piece in (grad_q, grad_k, grad_v)
        ]
    )
    grad_bqv = jnp.stack(
        [jnp.sum(grad_q, axis=0, dtype=jnp.float32), jnp.sum(grad_v, axis=0, dtype=jnp.float32)]
    )
    summed = jnp.zeros((local_rows * lax.axis_size("mp"), w_qkv.shape[1]), jnp.float32)
    for index, piece in enumerate((grad_q, grad_k, grad_v)):
        summed = summed + jnp.einsum(
            "tc,dc->td", piece, w_qkv[index], preferred_element_type=jnp.float32
        )
    grad_n1 = lax.psum_scatter(
        summed.astype(jnp.bfloat16), "mp", scatter_dimension=0, tiled=True
    ).astype(jnp.float32)
    grad_x, grad_g1, grad_s1 = first_back(grad_n1)
    grad_in = grad_x + grad_h
    weight_totals = (
        lax.psum(grad_qkv.astype(jnp.bfloat16), "dp").astype(jnp.float32),
        lax.psum(grad_bqv.astype(jnp.bfloat16), "dp").astype(jnp.float32),
        lax.psum(grad_wout.astype(jnp.bfloat16), "dp").astype(jnp.float32),
        lax.psum(grad_bout.astype(jnp.bfloat16), "dp").astype(jnp.float32),
        lax.psum(grad_up.astype(jnp.bfloat16), "dp").astype(jnp.float32),
        lax.psum(grad_bup.astype(jnp.bfloat16), "dp").astype(jnp.float32),
        lax.psum(grad_down.astype(jnp.bfloat16), "dp").astype(jnp.float32),
        lax.psum(grad_bdown.astype(jnp.bfloat16), "dp").astype(jnp.float32),
    )
    norm_totals = lax.psum(
        (jnp.stack([grad_g1, grad_g2]), jnp.stack([grad_s1, grad_s2])), ("dp", "mp")
    )
    return (block_out, grad_in) + tuple(weight_totals) + tuple(norm_totals)


def solution(mesh):
    in_specs = (
        P(("dp", "mp"), None),
        P(("dp", "mp")),
        P(None, None, "mp"),
        P(None, "mp"),
        P("mp", None),
        P(),
        P(None, "mp"),
        P("mp"),
        P("mp", None),
        P(),
        P(),
        P(),
        P(("dp", "mp"), None),
    )
    out_specs = (
        P(("dp", "mp"), None),
        P(("dp", "mp"), None),
        P(None, None, "mp"),
        P(None, "mp"),
        P("mp", None),
        P(),
        P(None, "mp"),
        P("mp"),
        P("mp", None),
        P(),
        P(),
        P(),
    )
    return jax.shard_map(shards, mesh=mesh, in_specs=in_specs, out_specs=out_specs, check_vma=False)
```

profile of v0, /device:TPU:0, one launch (start us, length us, event | category | flops | bytes accessed | tf_op | source)
XLA Modules:
  0.0 795.8 jit_solution(3557118762227939732)
XLA Ops:
  12.7 2.6 fusion.29
  15.4 6.2 all-gather
  25.2 27.5 %all-gather.6.cloned.1.call-done = bf16[2048,1024]{1,0:T(8,128)(2,1)} async-done(((bf16[512,1024]{1,0:T(8,128)(2,1)}), bf16[2048,1024]{1,0:T(8,128)(2,1)}) %all-gather.6.cloned.1.call-update) | async-done | bytes 4194320 | tf_op jit(solution)/shard_map/all_gather | solution.py:133
  52.7 3.6 fusion.22
  58.2 4.0 copy.62
  62.3 3.6 fusion.23
  67.6 3.2 fusion.83
  74.5 3.6 convolution_convert_fusion.4
  79.8 2.9 copy.66
  82.8 3.2 fusion.89
  91.0 3.5 fusion.88
  94.5 3.4 fusion
  100.2 4.0 fusion.55
  106.7 3.3 convolution_convert_fusion
  110.7 44.1 %reduce-scatter.5.cloned.1.call-done = bf16[512,1024]{1,0:T(8,128)(2,1)} async-done(((bf16[2048,1024]{1,0:T(8,128)(2,1)}), bf16[512,1024]{1,0:T(8,128)(2,1)}) %reduce-scatter.5.cloned.1.call-update) | async-done | bytes 1048592 | tf_op jit(solution)/shard_map/reduce_scatter | solution.py:145
  160.6 34.0 %all-gather.8.cloned.1.call-done = bf16[2048,1024]{1,0:T(8,128)(2,1)} async-done(((bf16[512,1024]{1,0:T(8,128)(2,1)}), bf16[2048,1024]{1,0:T(8,128)(2,1)}) %all-gather.8.cloned.1.call-update) | async-done | bytes 4194320 | tf_op jit(solution)/shard_map/all_gather | solution.py:154
  194.6 11.3 %fusion.91 = f32[2048,1024]{1,0:T(8,128)} fusion(bf16[2048,1024]{1,0:T(8,128)(2,1)} %all-gather.8.cloned.1.call-done, bf16[1024,1024]{1,0:T(8,128)(2,1)} %param.19), kind=kOutput, calls=%fused_computation.163 | convolution fusion | flops 4294967296 | bytes 14680064 | tf_op jit(solution)/shard_map/dot_general | solution.py:155
  205.9 24.6 %all-gather.10.cloned.1.call-done = bf16[2048,1024]{1,0:T(8,128)(2,1)} async-done(((bf16[512,1024]{1,0:T(8,128)(2,1)}), bf16[2048,1024]{1,0:T(8,128)(2,1)}) %all-gather.10.cloned.1.call-update) | async-done | bytes 4194320 | tf_op jit(solution)/shard_map/all_gather | solution.py:168
  230.5 27.5 %fusion.78 = (bf16[1024]{0:T(1024)(128)(2,1)S(1)}, bf16[2048,1024]{1,0:T(8,128)(2,1)S(1)}, f32[2048,1024]{1,0:T(8,128)}) fusion(f32[2048,1024]{1,0:T(8,128)} %fusion.91, f32[1024]{0:T(1024)S(1)} %convert_element_type.188, bf16[2048,1024]{1,0:T(8,128)(2,1)} %all-gather.10.cloned.1.call-done, bf16[1024,1024]{1,0:T(8,128)(2,1)S(1)} %copy-done), kind=kOutput, calls=%fused_computation.151 | convolution fusion | flops 4450155520 | bytes 27269120 | tf_op jit(solution)/shard_map/td,fd->tf/dot_general | solution.py:171
  260.0 6.2 convolution_convert_fusion.1
  266.3 10.4 %multiply_convert_fusion.2 = bf16[2048,1024]{1,0:T(8,128)(2,1)} fusion(f32[2048,1024]{1,0:T(8,128)} %get-tuple-element.31, f32[2048,1024]{1,0:T(8,128)} %fusion.91, f32[1024]{0:T(1024)S(1)} %convert_element_type.188), kind=kLoop, calls=%fused_computation.17 | loop fusion | flops 8388608 | bytes 20975616 | tf_op jit(solution)/shard_map/convert_element_type | solution.py:156
  276.7 8.4 %convolution_convert_fusion.2 = bf16[2048,1024]{1,0:T(8,128)(2,1)} fusion(bf16[2048,1024]{1,0:T(8,128)(2,1)} %multiply_convert_fusion.2, bf16[1024,1024]{1,0:T(8,128)(2,1)S(1)} %copy-done), kind=kOutput, calls=%fused_computation.43 | convolution fusion | flops 4297064448 | bytes 10485760 | tf_op jit(solution)/shard_map/dot_general | solution.py:160
  285.7 25.2 %reduce-scatter.9.cloned.1.call-done = bf16[512,1024]{1,0:T(8,128)(2,1)} async-done(((bf16[2048,1024]{1,0:T(8,128)(2,1)}), bf16[512,1024]{1,0:T(8,128)(2,1)}) %reduce-scatter.9.cloned.1.call-update) | async-done | bytes 1048592 | tf_op jit(solution)/shard_map/reduce_scatter | solution.py:176
  313.3 44.7 %reduce-scatter.7.cloned.1.call-done = bf16[512,1024]{1,0:T(8,128)(2,1)} async-done(((bf16[2048,1024]{1,0:T(8,128)(2,1)}), bf16[512,1024]{1,0:T(8,128)(2,1)}) %reduce-scatter.7.cloned.1.call-update) | async-done | bytes 1048592 | tf_op jit(solution)/shard_map/reduce_scatter | solution.py:159
  358.0 3.7 fusion.81
  364.5 9.5 %convolution_convert_fusion.6 = bf16[1024,1024]{1,0:T(8,128)(2,1)} fusion(bf16[2048,1024]{1,0:T(8,128)(2,1)} %all-gather.8.cloned.1.call-done, bf16[2048,1024]{1,0:T(8,128)(2,1)} %copy-done.55), kind=kOutput, calls=%fused_computation.90 | convolution fusion | flops 4296015872 | bytes 10485760 | tf_op jit(solution)/shard_map/td,tf->df/dot_general | solution.py:174
  374.0 6.0 convolution_convert_fusion.5
  379.9 19.0 %all-gather.12.cloned.1.call-done = bf16[2048,1024]{1,0:T(8,128)(2,1)} async-done(((bf16[512,1024]{1,0:T(8,128)(2,1)}), bf16[2048,1024]{1,0:T(8,128)(2,1)}) %all-gather.12.cloned.1.call-update) | async-done | bytes 4194320 | tf_op jit(solution)/shard_map/all_gather | solution.py:186
  398.9 4.5 convolution_convert_fusion.3
  403.4 3.3 reshape.222
  410.4 5.9 fusion.42
  416.3 4.6 multiply_reduce_fusion.1
  429.7 14.7 %multiply_reduce_fusion = (f32[2,4,512]{2,1,0:T(4,128)S(1)}, f32[2,4,512,1024]{3,2,1,0:T(8,128)}) fusion(f32[2,4,512,1024]{3,2,1,0:T(8,128)} %copy-done.2, f32[2,4,512]{2,1,0:T(4,128)S(1)} %bitcast.140, bf16[2,512,4,64]{1,3,2,0:T(8,128)(2,1)} %copy.98, bf16[2,1024,4,64]{1,3,2,0:T(8,128)(2,1)S(1)} %copy-done.15), kind=kOutput, calls=%fused_computation.1 | convolution fusion | flops 549449728 | bytes 35160064 | tf_op jit(solution)/shard_map/rqhd,rkhd->rhqk/dot_general | solution.py:79
  444.4 7.8 fusion.90
  453.6 10.9 %multiply_convert_fusion = bf16[2,4,512,1024]{3,2,1,0:T(8,128)(2,1)} fusion(f32[2,4,512,1024]{3,2,1,0:T(8,128)} %get-tuple-element.54, f32[2,4,512,1024]{3,2,1,0:T(8,128)S(1)} %bitcast.125, f32[2,4,512]{2,1,0:T(4,128)S(1)} %get-tuple-element.53, f32[2,4,512]{2,1,0:T(4,128)S(1)} %bitcast.142), kind=kLoop, calls=%fused_computation | loop fusion | flops 16777216 | bytes 41975808 | tf_op jit(solution)/shard_map/convert_element_type | solution.py:83
  464.6 6.2 fusion.47
  488.1 3.4 add_convert_fusion
  491.6 2.9 reduce_sum.246
  494.6 2.9 reduce_sum.244
  497.5 23.2 %all-reduce.3 = (bf16[2,256]{1,0:T(2,128)(2,1)S(1)}, bf16[1024]{0:T(1024)(128)(2,1)S(1)}, bf16[1024]{0:T(1024)(128)(2,1)S(1)}, bf16[1024]{0:T(1024)(128)(2,1)S(1)}) all-reduce(bf16[2,256]{1,0:T(2,128)(2,1)S(1)} %pad_maximum_fusion.4, bf16[1024]{0:T(1024)(128)(2,1)S(1)} %reduce_sum.244, ...), channel_id=1, replica_groups=mesh['dp'=8,'mp'=4] {'dp'}, use_global_device_ids=true, to_apply=%region_21.22 | all-reduce | flops 3584 | bytes 14336 | tf_op jit(solution)/shard_map/psum | solution.py:214
  523.1 171.2 %all-reduce.7.cloned.1.call-done = (bf16[3,1024,256]{2,1,0:T(8,128)(2,1)}, bf16[256,1024]{1,0:T(8,128)(2,1)}, bf16[1024,1024]{1,0:T(8,128)(2,1)}, bf16[1024,1024]{1,0:T(8,128)(2,1)}) async-done(((bf16[3,1024,256]{2,1,0:T(8,128)(2,1)}, bf16[256,1024]{1,0:T(8,128)(2,1)}, bf16[1024,1024]{1,0:T(8,128)(2,1)}, bf16[1024,1024]{1,0:T(8,128)(2,1)}), (bf16[3,1024,256]{2,1,0:T(8,128)(2,1)}, ...) | async-done | bytes 6291472 | tf_op jit(solution)/shard_map/psum | solution.py:213
  696.6 3.3 convert_element_type.212
  700.0 2.5 convert_element_type.220
  702.5 2.9 convert_element_type.223
  705.4 35.1 %reduce-scatter.11.cloned.1.call-done = bf16[512,1024]{1,0:T(8,128)(2,1)} async-done(((bf16[2048,1024]{1,0:T(8,128)(2,1)}), bf16[512,1024]{1,0:T(8,128)(2,1)}) %reduce-scatter.11.cloned.1.call-update) | async-done | bytes 1048592 | tf_op jit(solution)/shard_map/reduce_scatter | solution.py:207
  742.5 2.6 fusion.35
  745.1 39.5 %all-reduce.2 = (f32[2,1024]{1,0:T(2,128)}, f32[2,1024]{1,0:T(2,128)}) all-reduce(f32[2,1024]{1,0:T(2,128)S(1)} %get-tuple-element.59, f32[2,1024]{1,0:T(2,128)S(1)} %get-tuple-element.60), channel_id=1, replica_groups=mesh['dp'=8,'mp'=4] {'dp','mp'}, use_global_device_ids=true, to_apply=%region_33.34 | all-reduce | flops 4096 | bytes 32768 | tf_op jit(solution)/shard_map/psum | solution.py:222
  784.5 4.5 add_add_fusion.2
  (216 shorter events, 79.7 us)
Async XLA Ops:
  7.2 223.3 %copy-start = (bf16[1024,1024]{1,0:T(8,128)(2,1)S(1)}, bf16[1024,1024]{1,0:T(8,128)(2,1)}, u32[]{:S(2)}) copy-start(bf16[1024,1024]{1,0:T(8,128)(2,1)} %param.21) | copy-start | bytes 6291460
  7.2 8.2 %copy-start.49 = (s32[512]{0:T(512)S(1)}, s32[512]{0:T(512)}, u32[]{:S(2)}) copy-start(s32[512]{0:T(512)} %param.14) | copy-start | bytes 6148
  7.2 14.5 %copy-start.48 = (bf16[2,256]{1,0:T(2,128)(2,1)S(1)}, bf16[2,256]{1,0:T(2,128)(2,1)}, u32[]{:S(2)}) copy-start(bf16[2,256]{1,0:T(2,128)(2,1)} %param.16) | copy-start | bytes 3076
  7.2 45.5 %all-gather.6.cloned.1.call-start = ((), (), s32[]{:S(2)}) async-start(), calls=%async_computation.4 | async-start | bytes 5242880 | tf_op jit(solution)/shard_map/all_gather | solution.py:133
  8.8 12.9 %copy-start.40 = (f32[512]{0:T(512)}, f32[512]{0:T(512)S(1)}, u32[]{:S(2)}) copy-start(f32[512]{0:T(512)S(1)} %broadcast_multiply_fusion.1) | copy-start | bytes 6148
  11.1 4.3 copy-start.44
  11.9 9.9 %copy-start.38 = (f32[1,1024]{1,0:T(1,128)}, f32[1,1024]{1,0:T(1,128)S(1)}, u32[]{:S(2)}) copy-start(f32[1,1024]{1,0:T(1,128)S(1)} %get-tuple-element.43) | copy-start | bytes 12292
  15.3 139.4 %reduce-scatter.5.cloned.1.call-start = ((), (), s32[]{:S(2)}) async-start(), calls=%async_computation.5 | async-start | bytes 5242880 | tf_op jit(solution)/shard_map/reduce_scatter | solution.py:145
  82.8 8.2 %copy-start.9 = (bf16[2,1024,4,64]{1,3,2,0:T(8,128)(2,1)}, bf16[2,1024,4,64]{1,3,2,0:T(8,128)(2,1)S(1)}, u32[]{:S(2)}) copy-start(bf16[2,1024,4,64]{1,3,2,0:T(8,128)(2,1)S(1)} %copy.66) | copy-start | bytes 3145732
  86.0 3.4 copy-start.3
  86.0 3.4 copy-start.36
  86.0 3.4 copy-start.14
  94.5 5.7 copy-start.2
  110.0 44.8 %copy-start.4 = (bf16[512,1024]{1,0:T(8,128)(2,1)S(1)}, bf16[512,1024]{1,0:T(8,128)(2,1)}, u32[]{:S(2)}) copy-start(bf16[512,1024]{1,0:T(8,128)(2,1)} %param.13) | copy-start | bytes 3145732
  110.0 84.5 %all-gather.8.cloned.1.call-start = ((), (), s32[]{:S(2)}) async-start(), calls=%async_computation.6 | async-start | bytes 5242880 | tf_op jit(solution)/shard_map/all_gather | solution.py:154
  154.8 3.6 copy-start.6
  156.5 4.1 copy-start.51
  159.9 70.5 %all-gather.10.cloned.1.call-start = ((), (), s32[]{:S(2)}) async-start(), calls=%async_computation.8 | async-start | bytes 5242880 | tf_op jit(solution)/shard_map/all_gather | solution.py:168
  160.5 150.5 %reduce-scatter.9.cloned.1.call-start = ((), (), s32[]{:S(2)}) async-start(), calls=%async_computation.9 | async-start | bytes 5242880 | tf_op jit(solution)/shard_map/reduce_scatter | solution.py:176
  230.5 29.5 %copy-start.54 = (bf16[1024,1024]{1,0:T(8,128)(2,1)S(1)}, bf16[1024,1024]{1,0:T(8,128)(2,1)}, u32[]{:S(2)}) copy-start(bf16[1024,1024]{1,0:T(8,128)(2,1)} %param.19) | copy-start | bytes 6291460
  266.2 91.7 %reduce-scatter.7.cloned.1.call-start = ((), (), s32[]{:S(2)}) async-start(), calls=%async_computation.7 | async-start | bytes 5242880 | tf_op jit(solution)/shard_map/reduce_scatter | solution.py:159
  285.1 25.9 %copy-start.7 = (bf16[512,1024]{1,0:T(8,128)(2,1)S(1)}, bf16[512,1024]{1,0:T(8,128)(2,1)}, u32[]{:S(2)}) copy-start(bf16[512,1024]{1,0:T(8,128)(2,1)} %reduce-scatter.5.cloned.1.call-done) | copy-start | bytes 3145732
  285.1 113.9 %all-gather.12.cloned.1.call-start = ((), (), s32[]{:S(2)}) async-start(), calls=%async_computation.10 | async-start | bytes 5242880 | tf_op jit(solution)/shard_map/all_gather | solution.py:186
  313.3 49.7 %copy-start.11 = (bf16[512,1024]{1,0:T(8,128)(2,1)S(1)}, bf16[512,1024]{1,0:T(8,128)(2,1)}, u32[]{:S(2)}) copy-start(bf16[512,1024]{1,0:T(8,128)(2,1)} %param.25) | copy-start | bytes 3145732
  364.3 330.0 %all-reduce.7.cloned.1.call-start = ((), (), s32[]{:S(2)}) async-start(), calls=%async_computation.12 | async-start | bytes 12582912 | tf_op jit(solution)/shard_map/psum | solution.py:213
  364.4 9.5 %copy-start.26 = (bf16[2048,1024]{1,0:T(8,128)(2,1)S(1)}, bf16[2048,1024]{1,0:T(8,128)(2,1)}, u32[]{:S(2)}) copy-start(bf16[2048,1024]{1,0:T(8,128)(2,1)} %all-gather.10.cloned.1.call-done) | copy-start | bytes 12582916
  364.4 9.5 %copy-start.28 = (bf16[2048,1024]{1,0:T(8,128)(2,1)S(1)}, bf16[2048,1024]{1,0:T(8,128)(2,1)}, u32[]{:S(2)}) copy-start(bf16[2048,1024]{1,0:T(8,128)(2,1)} %multiply_convert_fusion.2) | copy-start | bytes 12582916
  374.0 25.0 %copy-start.35 = (bf16[256,1024]{1,0:T(8,128)(2,1)S(1)}, bf16[256,1024]{1,0:T(8,128)(2,1)}, u32[]{:S(2)}) copy-start(bf16[256,1024]{1,0:T(8,128)(2,1)} %param.17) | copy-start | bytes 1572868
  410.4 5.9 copy-start.15
  410.4 10.5 %slice-start.4 = ((s8[8388608]{0:T(1024)(128)(4,1)}), s8[4194304]{0:T(1024)(128)(4,1)S(1)}, s32[]{:S(2)}) async-start(s8[8388608]{0:T(1024)(128)(4,1)} %bitcast.126), calls=%async_computation.17 | async-start | bytes 8388608
  416.3 4.6 slice-start.5
  429.6 14.7 %copy-start.20 = (bf16[2,512,4,64]{1,3,2,0:T(8,128)(2,1)S(1)}, bf16[2,512,4,64]{1,3,2,0:T(8,128)(2,1)}, u32[]{:S(2)}) copy-start(bf16[2,512,4,64]{1,3,2,0:T(8,128)(2,1)} %copy.98) | copy-start | bytes 1572868
  429.6 14.7 %copy-start.22 = (f32[2,512,4,64]{1,3,2,0:T(8,128)S(1)}, f32[2,512,4,64]{1,3,2,0:T(8,128)}, u32[]{:S(2)}) copy-start(f32[2,512,4,64]{1,3,2,0:T(8,128)} %fusion.42) | copy-start | bytes 3145732
  429.6 23.9 %slice-start = ((s8[16777216]{0:T(1024)(128)(4,1)}), s8[4194304]{0:T(1024)(128)(4,1)S(1)}, s32[]{:S(2)}) async-start(s8[16777216]{0:T(1024)(128)(4,1)} %bitcast.124), calls=%async_computation.13 | async-start | bytes 8388608
  429.6 23.9 %slice-start.1 = ((s8[16777216]{0:T(1024)(128)(4,1)}), s8[4194304]{0:T(1024)(128)(4,1)S(1)}, s32[]{:S(2)}) async-start(s8[16777216]{0:T(1024)(128)(4,1)} %bitcast.124), calls=%async_computation.14 | async-start | bytes 8388608
  429.6 23.9 %slice-start.2 = ((s8[16777216]{0:T(1024)(128)(4,1)}), s8[4194304]{0:T(1024)(128)(4,1)S(1)}, s32[]{:S(2)}) async-start(s8[16777216]{0:T(1024)(128)(4,1)} %bitcast.124), calls=%async_computation.15 | async-start | bytes 8388608
  444.4 9.2 %slice-start.3 = ((s8[16777216]{0:T(1024)(128)(4,1)}), s8[4194304]{0:T(1024)(128)(4,1)S(1)}, s32[]{:S(2)}) async-start(s8[16777216]{0:T(1024)(128)(4,1)} %bitcast.124), calls=%async_computation.16 | async-start | bytes 8388608
  453.5 21.8 %copy-start.23 = (bf16[32,8,2,1024]{3,1,2,0:T(8,128)(2,1)}, bf16[32,8,2,1024]{3,1,2,0:T(8,128)(2,1)S(1)}, u32[]{:S(2)}) copy-start(bf16[32,8,2,1024]{3,1,2,0:T(8,128)(2,1)S(1)} %copy.102) | copy-start | bytes 3145732
  464.5 6.2 copy-start.5
  464.5 6.2 copy-start.17
  464.6 6.2 copy-start.29
  483.1 257.4 %reduce-scatter.11.cloned.1.call-start = ((), (), s32[]{:S(2)}) async-start(), calls=%async_computation.11 | async-start | bytes 5242880 | tf_op jit(solution)/shard_map/reduce_scatter | solution.py:207
  694.3 5.6 copy-start.31
  702.4 38.1 %copy-start.39 = (f32[1,1024]{1,0:T(1,128)S(1)}, f32[1,1024]{1,0:T(1,128)}, u32[]{:S(2)}) copy-start(f32[1,1024]{1,0:T(1,128)} %copy-done.38) | copy-start | bytes 12292
  702.4 38.1 %copy-start.41 = (f32[512]{0:T(512)S(1)}, f32[512]{0:T(512)}, u32[]{:S(2)}) copy-start(f32[512]{0:T(512)} %copy-done.40) | copy-start | bytes 6148
  702.4 40.0 %copy-start.47 = (f32[512]{0:T(512)S(1)}, f32[512]{0:T(512)}, u32[]{:S(2)}) copy-start(f32[512]{0:T(512)} %copy-done.46) | copy-start | bytes 6148
  702.4 40.0 %copy-start.45 = (f32[512]{0:T(512)S(1)}, f32[512]{0:T(512)}, u32[]{:S(2)}) copy-start(f32[512]{0:T(512)} %copy-done.44) | copy-start | bytes 6148
  742.5 46.6 %copy-start.1 = (bf16[1024,1024]{1,0:T(8,128)(2,1)S(1)}, bf16[1024,1024]{1,0:T(8,128)(2,1)}, u32[]{:S(2)}) copy-start(bf16[1024,1024]{1,0:T(8,128)(2,1)} %param.21) | copy-start | bytes 6291460
  (23 other events, 43.0 us)
Sparse Core Ops, SparseCore 0:
  15.5 37.1 all-gather.5
  110.2 44.5 reduce-scatter.4
  160.0 34.4 all-gather.7
  196.0 34.4 all-gather.9
  266.4 44.5 reduce-scatter.8
  313.4 44.5 reduce-scatter.6
  364.5 34.4 all-gather.11
  483.2 211.0 all-reduce.6
  696.9 43.6 reduce-scatter.10
where the time goes:
time: 801 us; the launch traced here: 796 us
  waiting for transfers between devices  426 us (53%)
  matrix products  158 us (20%)
  other arithmetic  80 us (10%)
  blocking collectives  68.8 us (9%)
  local copies, waits for them, and re-layouts  47.6 us (6%)
  between operations  14.9 us (2%)
    psum x1, waiting for transfers between devices, shards(): lax.psum(grad_qkv.astype(jnp.bfloat16), 'dp').astype(jnp.float32)  171 us
    reduce_scatter x1, waiting for transfers between devices, shards(): lax.psum_scatter(jnp.dot(activ, w_down, preferred_element_type=jnp.float3...  44.7 us
    reduce_scatter x1, waiting for transfers between devices, shards(): lax.psum_scatter(jnp.dot(attended, w_out, preferred_element_type=jnp.floa...  44.1 us
    psum x1, blocking collectives, shards(): lax.psum((jnp.stack([grad_g1, grad_g2]), jnp.stack([grad_s1, grad_s2])),...  39.5 us
    reduce_scatter x1, waiting for transfers between devices, shards(): lax.psum_scatter(summed.astype(jnp.bfloat16), 'mp', scatter_dimension=0,...  35.1 us
    all_gather x1, waiting for transfers between devices, shards(): joined2 = lax.all_gather(lowered2, 'mp', axis=0, tiled=True)  34 us
    dot_general x1, matrix products, shards(): jnp.einsum('td,fd->tf', grad_z, w_down, preferred_element_type=jnp.float32)  27.5 us
    all_gather x1, waiting for transfers between devices, shards(): lax.all_gather(lowered, 'mp', axis=0, tiled=True)  27.5 us
  transfers between devices with their start and end apart: 9, of which 9 were waited for; matrix products, arithmetic and copies ran while one was open for 10% of the time, Pallas kernels for 0%

commit v1 on v0

--- a/solution.py
+++ b/solution.py
@@ -210,7 +210,7 @@
     grad_x, grad_g1, grad_s1 = first_back(grad_n1)
     grad_in = grad_x + grad_h
     weight_totals = (
-        lax.psum(grad_qkv.astype(jnp.bfloat16), "dp").astype(jnp.float32),
+        jnp.sum(lax.all_gather(grad_qkv.astype(jnp.bfloat16), "dp"), axis=0).astype(jnp.float32),
         lax.psum(grad_bqv.astype(jnp.bfloat16), "dp").astype(jnp.float32),
         lax.psum(grad_wout.astype(jnp.bfloat16), "dp").astype(jnp.float32),
         lax.psum(grad_bout.astype(jnp.bfloat16), "dp").astype(jnp.float32),

time: 801 us -> 878 us (1.096)
  waiting for transfers between devices: 426 us -> 486 us
  other arithmetic: 80 us -> 93.2 us
    all_gather x0 -> x1, waiting for transfers between devices: none -> 127 us  [shards(): lax.all_gather(grad_qkv.astype(jnp.bfloat16), 'dp')]
    psum x1, waiting for transfers between devices: 171 us -> 103 us  [shards(): lax.psum(grad_wout.astype(jnp.bfloat16), 'dp').astype(jnp.float32)]
    unnamed x132 -> x116, local copies, waits for them, and re-layouts: 20.4 us -> 22.7 us
  transfers between devices with their start and end apart: 9 -> 10, of which waited for: 9 -> 10; matrix products, arithmetic and copies ran while one was open for 10% -> 13% of each run, Pallas kernels for 0% -> 0%
where the time goes in v1:
time: 878 us; the launch traced here: 873 us
  waiting for transfers between devices  486 us (55%)
  matrix products  155 us (18%)
  other arithmetic  93.2 us (11%)
  blocking collectives  73 us (8%)
  local copies, waits for them, and re-layouts  49.9 us (6%)
  between operations  15.2 us (2%)
    all_gather x1, waiting for transfers between devices, shards(): lax.all_gather(grad_qkv.astype(jnp.bfloat16), 'dp')  127 us
    psum x1, waiting for transfers between devices, shards(): lax.psum(grad_wout.astype(jnp.bfloat16), 'dp').astype(jnp.float32)  103 us
    reduce_scatter x1, waiting for transfers between devices, shards(): lax.psum_scatter(jnp.dot(activ, w_down, preferred_element_type=jnp.float3...  44.7 us
    psum x1, blocking collectives, shards(): lax.psum((jnp.stack([grad_g1, grad_g2]), jnp.stack([grad_s1, grad_s2])),...  44.4 us
    reduce_scatter x1, waiting for transfers between devices, shards(): lax.psum_scatter(jnp.dot(attended, w_out, preferred_element_type=jnp.floa...  44.1 us
    reduce_scatter x1, waiting for transfers between devices, shards(): lax.psum_scatter(summed.astype(jnp.bfloat16), 'mp', scatter_dimension=0,...  37.1 us
    all_gather x1, waiting for transfers between devices, shards(): joined2 = lax.all_gather(lowered2, 'mp', axis=0, tiled=True)  34 us
    all_gather x1, waiting for transfers between devices, shards(): lax.all_gather(lowered, 'mp', axis=0, tiled=True)  27.5 us
  transfers between devices with their start and end apart: 10, of which 10 were waited for; matrix products, arithmetic and copies ran while one was open for 13% of the time, Pallas kernels for 0%

profile of v1, /device:TPU:0, one launch (start us, length us, event | category | flops | bytes accessed | tf_op | source)
XLA Modules:
  0.0 873.0 jit_solution(8544774642151112982)
XLA Ops:
  15.4 6.2 all-gather
  25.2 27.5 %all-gather.7.cloned.1.call-done = bf16[2048,1024]{1,0:T(8,128)(2,1)} async-done(((bf16[512,1024]{1,0:T(8,128)(2,1)}), bf16[2048,1024]{1,0:T(8,128)(2,1)}) %all-gather.7.cloned.1.call-update) | async-done | bytes 4194320 | tf_op jit(solution)/shard_map/all_gather | solution.py:133
  52.7 3.6 fusion.22
  58.2 4.0 copy.62
  62.2 3.6 fusion.23
  67.6 3.2 fusion.83
  74.5 3.6 convolution_convert_fusion.4
  79.8 2.9 copy.66
  82.8 3.2 fusion.89
  91.0 3.5 fusion.88
  94.5 3.4 fusion
  100.2 4.0 fusion.55
  106.7 3.3 convolution_convert_fusion
  110.7 44.1 %reduce-scatter.5.cloned.1.call-done = bf16[512,1024]{1,0:T(8,128)(2,1)} async-done(((bf16[2048,1024]{1,0:T(8,128)(2,1)}), bf16[512,1024]{1,0:T(8,128)(2,1)}) %reduce-scatter.5.cloned.1.call-update) | async-done | bytes 1048592 | tf_op jit(solution)/shard_map/reduce_scatter | solution.py:145
  160.6 34.0 %all-gather.9.cloned.1.call-done = bf16[2048,1024]{1,0:T(8,128)(2,1)} async-done(((bf16[512,1024]{1,0:T(8,128)(2,1)}), bf16[2048,1024]{1,0:T(8,128)(2,1)}) %all-gather.9.cloned.1.call-update) | async-done | bytes 4194320 | tf_op jit(solution)/shard_map/all_gather | solution.py:154
  194.6 11.3 %fusion.91 = f32[2048,1024]{1,0:T(8,128)} fusion(bf16[2048,1024]{1,0:T(8,128)(2,1)} %all-gather.9.cloned.1.call-done, bf16[1024,1024]{1,0:T(8,128)(2,1)} %param.19), kind=kOutput, calls=%fused_computation.163 | convolution fusion | flops 4294967296 | bytes 14680064 | tf_op jit(solution)/shard_map/dot_general | solution.py:155
  205.9 24.6 %all-gather.11.cloned.1.call-done = bf16[2048,1024]{1,0:T(8,128)(2,1)} async-done(((bf16[512,1024]{1,0:T(8,128)(2,1)}), bf16[2048,1024]{1,0:T(8,128)(2,1)}) %all-gather.11.cloned.1.call-update) | async-done | bytes 4194320 | tf_op jit(solution)/shard_map/all_gather | solution.py:168
  230.5 27.4 %fusion.78 = (bf16[1024]{0:T(1024)(128)(2,1)S(1)}, bf16[2048,1024]{1,0:T(8,128)(2,1)S(1)}, f32[2048,1024]{1,0:T(8,128)}) fusion(f32[2048,1024]{1,0:T(8,128)} %fusion.91, f32[1024]{0:T(1024)S(1)} %convert_element_type.197, bf16[2048,1024]{1,0:T(8,128)(2,1)} %all-gather.11.cloned.1.call-done, bf16[1024,1024]{1,0:T(8,128)(2,1)S(1)} %copy-done), kind=kOutput, calls=%fused_computation.151 | convolution fusion | flops 4450155520 | bytes 27269120 | tf_op jit(solution)/shard_map/td,fd->tf/dot_general | solution.py:171
  259.8 6.2 convolution_convert_fusion.1
  266.1 10.4 %multiply_convert_fusion.2 = bf16[2048,1024]{1,0:T(8,128)(2,1)} fusion(f32[2048,1024]{1,0:T(8,128)} %get-tuple-element.30, f32[2048,1024]{1,0:T(8,128)} %fusion.91, f32[1024]{0:T(1024)S(1)} %convert_element_type.197), kind=kLoop, calls=%fused_computation.17 | loop fusion | flops 8388608 | bytes 20975616 | tf_op jit(solution)/shard_map/convert_element_type | solution.py:156
  276.5 8.4 convolution_convert_fusion.2
  285.6 25.2 %reduce-scatter.9.cloned.1.call-done = bf16[512,1024]{1,0:T(8,128)(2,1)} async-done(((bf16[2048,1024]{1,0:T(8,128)(2,1)}), bf16[512,1024]{1,0:T(8,128)(2,1)}) %reduce-scatter.9.cloned.1.call-update) | async-done | bytes 1048592 | tf_op jit(solution)/shard_map/reduce_scatter | solution.py:176
  313.1 44.7 %reduce-scatter.7.cloned.1.call-done = bf16[512,1024]{1,0:T(8,128)(2,1)} async-done(((bf16[2048,1024]{1,0:T(8,128)(2,1)}), bf16[512,1024]{1,0:T(8,128)(2,1)}) %reduce-scatter.7.cloned.1.call-update) | async-done | bytes 1048592 | tf_op jit(solution)/shard_map/reduce_scatter | solution.py:159
  357.8 3.7 fusion.81
  364.3 9.5 %convolution_convert_fusion.6 = bf16[1024,1024]{1,0:T(8,128)(2,1)} fusion(bf16[2048,1024]{1,0:T(8,128)(2,1)} %all-gather.9.cloned.1.call-done, bf16[2048,1024]{1,0:T(8,128)(2,1)} %copy-done.51), kind=kOutput, calls=%fused_computation.90 | convolution fusion | flops 4296015872 | bytes 10485760 | tf_op jit(solution)/shard_map/td,tf->df/dot_general | solution.py:174
  373.8 6.0 convolution_convert_fusion.5
  379.8 19.0 %all-gather.13.cloned.1.call-done = bf16[2048,1024]{1,0:T(8,128)(2,1)} async-done(((bf16[512,1024]{1,0:T(8,128)(2,1)}), bf16[2048,1024]{1,0:T(8,128)(2,1)}) %all-gather.13.cloned.1.call-update) | async-done | bytes 4194320 | tf_op jit(solution)/shard_map/all_gather | solution.py:186
  398.8 4.5 convolution_convert_fusion.3
  403.2 3.3 reshape.270
  410.2 5.8 fusion.42
  416.0 6.3 multiply_reduce_fusion.1
  423.9 13.3 %multiply_reduce_fusion = (f32[2,4,512]{2,1,0:T(4,128)S(1)}, f32[2,4,512,1024]{3,2,1,0:T(8,128)}) fusion(f32[2,4,512,1024]{3,2,1,0:T(8,128)} %copy-done.2, f32[2,4,512]{2,1,0:T(4,128)S(1)} %bitcast.138, bf16[2,512,4,64]{1,3,2,0:T(8,128)(2,1)S(1)} %copy.98, bf16[2,1024,4,64]{1,3,2,0:T(8,128)(2,1)S(1)} %copy-done.17), kind=kOutput, calls=%fused_computation.1 | convolution fusion | flops 549449728 | bytes 35160064 | tf_op jit(solution)/shard_map/rqhd,rkhd->rhqk/dot_general | solution.py:79
  437.2 7.6 fusion.90
  447.2 4.7 multiply_convert_fusion.1
  459.0 13.3 %multiply_convert_fusion = bf16[2,4,512,1024]{3,2,1,0:T(8,128)(2,1)S(1)} fusion(f32[2,4,512,1024]{3,2,1,0:T(8,128)} %get-tuple-element.53, f32[2,4,512,1024]{3,2,1,0:T(8,128)} %copy-done.2, f32[2,4,512]{2,1,0:T(4,128)S(1)} %get-tuple-element.52, f32[2,4,512]{2,1,0:T(4,128)S(1)} %bitcast.140), kind=kLoop, calls=%fused_computation | loop fusion | flops 16777216 | bytes 41975808 | tf_op jit(solution)/shard_map/convert_element_type | solution.py:83
  483.9 3.3 add_convert_fusion
  487.5 4.0 fusion.54
  495.5 2.9 reduce_sum.259
  498.5 3.0 reduce_sum.257
  501.5 22.5 %all-reduce.3 = (bf16[2,256]{1,0:T(2,128)(2,1)S(1)}, bf16[1024]{0:T(1024)(128)(2,1)S(1)}, bf16[1024]{0:T(1024)(128)(2,1)S(1)}, bf16[1024]{0:T(1024)(128)(2,1)S(1)}) all-reduce(bf16[2,256]{1,0:T(2,128)(2,1)S(1)} %pad_maximum_fusion.4, bf16[1024]{0:T(1024)(128)(2,1)S(1)} %reduce_sum.257, ...), channel_id=1, replica_groups=mesh['dp'=8,'mp'=4] {'dp'}, use_global_device_ids=true, to_apply=%region_21.22 | all-reduce | flops 3584 | bytes 14336 | tf_op jit(solution)/shard_map/psum | solution.py:214
  526.4 102.9 %all-reduce.7.cloned.1.call-done = (bf16[256,1024]{1,0:T(8,128)(2,1)}, bf16[1024,1024]{1,0:T(8,128)(2,1)}, bf16[1024,1024]{1,0:T(8,128)(2,1)}) async-done(((bf16[256,1024]{1,0:T(8,128)(2,1)}, bf16[1024,1024]{1,0:T(8,128)(2,1)}, bf16[1024,1024]{1,0:T(8,128)(2,1)}), (bf16[256,1024]{1,0:T(8,128)(2,1)}, bf16[1024,1024]{1,0:T(8,128)(2,1)}, bf16[1024,1024]{1,0:T(8,128)(2,1)})) %all-reduce.7.cloned.1.call-update) | async-done | bytes 4718608 | tf_op jit(solution)/shard_map/psum | solution.py:215
  631.6 4.1 convert_element_type.229
  638.3 37.1 %reduce-scatter.11.cloned.1.call-done = bf16[512,1024]{1,0:T(8,128)(2,1)} async-done(((bf16[2048,1024]{1,0:T(8,128)(2,1)}), bf16[512,1024]{1,0:T(8,128)(2,1)}) %reduce-scatter.11.cloned.1.call-update) | async-done | bytes 1048592 | tf_op jit(solution)/shard_map/reduce_scatter | solution.py:207
  679.8 44.4 %all-reduce.2 = (f32[2,1024]{1,0:T(2,128)}, f32[2,1024]{1,0:T(2,128)}) all-reduce(f32[2,1024]{1,0:T(2,128)S(1)} %get-tuple-element.58, f32[2,1024]{1,0:T(2,128)S(1)} %get-tuple-element.59), channel_id=1, replica_groups=mesh['dp'=8,'mp'=4] {'dp','mp'}, use_global_device_ids=true, to_apply=%region_33.34 | all-reduce | flops 4096 | bytes 32768 | tf_op jit(solution)/shard_map/psum | solution.py:222
  724.2 3.8 add_add_fusion.2
  728.0 126.6 %all-gather.15.cloned.1.call-done = bf16[8,3,1024,256]{3,2,1,0:T(8,128)(2,1)} async-done(((bf16[1,3,1024,256]{3,2,1,0:T(8,128)(2,1)}), bf16[8,3,1024,256]{3,2,1,0:T(8,128)(2,1)}) %all-gather.15.cloned.1.call-update) | async-done | bytes 12582928 | tf_op jit(solution)/shard_map/all_gather | solution.py:213
  854.6 8.0 reduce_sum.254
  862.6 3.3 convert_element_type.221
  (203 shorter events, 86.8 us)
Async XLA Ops:
  7.2 223.3 %copy-start = (bf16[1024,1024]{1,0:T(8,128)(2,1)S(1)}, bf16[1024,1024]{1,0:T(8,128)(2,1)}, u32[]{:S(2)}) copy-start(bf16[1024,1024]{1,0:T(8,128)(2,1)} %param.21) | copy-start | bytes 6291460
  7.2 8.2 copy-start.45
  7.2 14.5 %copy-start.44 = (bf16[2,256]{1,0:T(2,128)(2,1)S(1)}, bf16[2,256]{1,0:T(2,128)(2,1)}, u32[]{:S(2)}) copy-start(bf16[2,256]{1,0:T(2,128)(2,1)} %param.16) | copy-start | bytes 3076
  7.2 45.5 %all-gather.7.cloned.1.call-start = ((), (), s32[]{:S(2)}) async-start(), calls=%async_computation.4 | async-start | bytes 5242880 | tf_op jit(solution)/shard_map/all_gather | solution.py:133
  8.8 12.9 %copy-start.36 = (f32[512]{0:T(512)}, f32[512]{0:T(512)S(1)}, u32[]{:S(2)}) copy-start(f32[512]{0:T(512)S(1)} %broadcast_multiply_fusion.1) | copy-start | bytes 6148
  11.1 4.3 copy-start.40
  11.9 9.9 %copy-start.34 = (f32[1,1024]{1,0:T(1,128)}, f32[1,1024]{1,0:T(1,128)S(1)}, u32[]{:S(2)}) copy-start(f32[1,1024]{1,0:T(1,128)S(1)} %get-tuple-element.42) | copy-start | bytes 12292
  15.3 139.5 %reduce-scatter.5.cloned.1.call-start = ((), (), s32[]{:S(2)}) async-start(), calls=%async_computation.5 | async-start | bytes 5242880 | tf_op jit(solution)/shard_map/reduce_scatter | solution.py:145
  82.8 8.2 copy-start.11
  86.0 3.4 copy-start.3
  86.0 3.4 copy-start.32
  86.0 3.4 copy-start.16
  94.5 5.7 copy-start.2
  110.1 44.8 %copy-start.4 = (bf16[512,1024]{1,0:T(8,128)(2,1)S(1)}, bf16[512,1024]{1,0:T(8,128)(2,1)}, u32[]{:S(2)}) copy-start(bf16[512,1024]{1,0:T(8,128)(2,1)} %param.13) | copy-start | bytes 3145732
  110.1 84.5 %all-gather.9.cloned.1.call-start = ((), (), s32[]{:S(2)}) async-start(), calls=%async_computation.6 | async-start | bytes 5242880 | tf_op jit(solution)/shard_map/all_gather | solution.py:154
  154.8 3.6 copy-start.7
  156.5 4.1 copy-start.47
  160.0 70.5 %all-gather.11.cloned.1.call-start = ((), (), s32[]{:S(2)}) async-start(), calls=%async_computation.8 | async-start | bytes 5242880 | tf_op jit(solution)/shard_map/all_gather | solution.py:168
  160.5 150.3 %reduce-scatter.9.cloned.1.call-start = ((), (), s32[]{:S(2)}) async-start(), calls=%async_computation.9 | async-start | bytes 5242880 | tf_op jit(solution)/shard_map/reduce_scatter | solution.py:176
  230.5 29.3 %copy-start.50 = (bf16[1024,1024]{1,0:T(8,128)(2,1)S(1)}, bf16[1024,1024]{1,0:T(8,128)(2,1)}, u32[]{:S(2)}) copy-start(bf16[1024,1024]{1,0:T(8,128)(2,1)} %param.19) | copy-start | bytes 6291460
  266.1 91.7 %reduce-scatter.7.cloned.1.call-start = ((), (), s32[]{:S(2)}) async-start(), calls=%async_computation.7 | async-start | bytes 5242880 | tf_op jit(solution)/shard_map/reduce_scatter | solution.py:159
  284.9 25.9 %copy-start.8 = (bf16[512,1024]{1,0:T(8,128)(2,1)S(1)}, bf16[512,1024]{1,0:T(8,128)(2,1)}, u32[]{:S(2)}) copy-start(bf16[512,1024]{1,0:T(8,128)(2,1)} %reduce-scatter.5.cloned.1.call-done) | copy-start | bytes 3145732
  285.0 113.8 %all-gather.13.cloned.1.call-start = ((), (), s32[]{:S(2)}) async-start(), calls=%async_computation.10 | async-start | bytes 5242880 | tf_op jit(solution)/shard_map/all_gather | solution.py:186
  313.1 49.7 %copy-start.13 = (bf16[512,1024]{1,0:T(8,128)(2,1)S(1)}, bf16[512,1024]{1,0:T(8,128)(2,1)}, u32[]{:S(2)}) copy-start(bf16[512,1024]{1,0:T(8,128)(2,1)} %param.25) | copy-start | bytes 3145732
  361.5 2.7 copy-start.39
  364.1 265.1 %all-reduce.7.cloned.1.call-start = ((), (), s32[]{:S(2)}) async-start(), calls=%async_computation.13 | async-start | bytes 9437184 | tf_op jit(solution)/shard_map/psum | solution.py:215
  364.3 9.5 %copy-start.24 = (bf16[2048,1024]{1,0:T(8,128)(2,1)S(1)}, bf16[2048,1024]{1,0:T(8,128)(2,1)}, u32[]{:S(2)}) copy-start(bf16[2048,1024]{1,0:T(8,128)(2,1)} %all-gather.11.cloned.1.call-done) | copy-start | bytes 12582916
  364.3 9.5 %copy-start.26 = (bf16[2048,1024]{1,0:T(8,128)(2,1)S(1)}, bf16[2048,1024]{1,0:T(8,128)(2,1)}, u32[]{:S(2)}) copy-start(bf16[2048,1024]{1,0:T(8,128)(2,1)} %multiply_convert_fusion.2) | copy-start | bytes 12582916
  373.8 25.0 %copy-start.31 = (bf16[256,1024]{1,0:T(8,128)(2,1)S(1)}, bf16[256,1024]{1,0:T(8,128)(2,1)}, u32[]{:S(2)}) copy-start(bf16[256,1024]{1,0:T(8,128)(2,1)} %param.17) | copy-start | bytes 1572868
  410.2 5.9 copy-start.17
  423.9 23.3 %slice-start = ((s8[8388608]{0:T(1024)(128)(4,1)}), s8[4194304]{0:T(1024)(128)(4,1)S(1)}, s32[]{:S(2)}) async-start(s8[8388608]{0:T(1024)(128)(4,1)} %bitcast.124), calls=%async_computation.14 | async-start | bytes 8388608
  423.9 13.3 %copy-start.21 = (f32[2,512,4,64]{1,3,2,0:T(8,128)S(1)}, f32[2,512,4,64]{1,3,2,0:T(8,128)}, u32[]{:S(2)}) copy-start(f32[2,512,4,64]{1,3,2,0:T(8,128)} %fusion.42) | copy-start | bytes 3145732
  423.9 23.3 %slice-start.1 = ((s8[8388608]{0:T(1024)(128)(4,1)}), s8[4194304]{0:T(1024)(128)(4,1)S(1)}, s32[]{:S(2)}) async-start(s8[8388608]{0:T(1024)(128)(4,1)} %bitcast.124), calls=%async_computation.15 | async-start | bytes 8388608
  447.2 6.8 copy-start.20
  453.9 2.9 copy-start.25
  459.0 216.5 %reduce-scatter.11.cloned.1.call-start = ((), (), s32[]{:S(2)}) async-start(), calls=%async_computation.11 | async-start | bytes 5242880 | tf_op jit(solution)/shard_map/reduce_scatter | solution.py:207
  459.0 13.3 %copy-start.19 = (bf16[2,512,4,64]{1,3,2,0:T(8,128)(2,1)S(1)}, bf16[2,512,4,64]{1,3,2,0:T(8,128)(2,1)}, u32[]{:S(2)}) copy-start(bf16[2,512,4,64]{1,3,2,0:T(8,128)(2,1)} %copy.96) | copy-start | bytes 1572868
  459.0 13.3 %copy-start.27 = (f32[2,512,4,64]{1,3,2,0:T(8,128)S(1)}, f32[2,512,4,64]{1,3,2,0:T(8,128)}, u32[]{:S(2)}) copy-start(f32[2,512,4,64]{1,3,2,0:T(8,128)} %fusion.45) | copy-start | bytes 3145732
  472.4 3.1 copy-start.12
  487.2 367.4 %all-gather.15.cloned.1.call-start = ((), (), s32[]{:S(2)}) async-start(), calls=%async_computation.12 | async-start | bytes 14155776 | tf_op jit(solution)/shard_map/all_gather | solution.py:213
  487.5 4.0 copy-start.49
  629.3 6.4 copy-start.28
  635.6 39.8 %copy-start.35 = (f32[1,1024]{1,0:T(1,128)S(1)}, f32[1,1024]{1,0:T(1,128)}, u32[]{:S(2)}) copy-start(f32[1,1024]{1,0:T(1,128)} %copy-done.34) | copy-start | bytes 12292
  635.6 39.8 %copy-start.37 = (f32[512]{0:T(512)S(1)}, f32[512]{0:T(512)}, u32[]{:S(2)}) copy-start(f32[512]{0:T(512)} %copy-done.36) | copy-start | bytes 6148
  635.6 41.7 %copy-start.43 = (f32[512]{0:T(512)S(1)}, f32[512]{0:T(512)}, u32[]{:S(2)}) copy-start(f32[512]{0:T(512)} %copy-done.42) | copy-start | bytes 6148
  635.6 41.7 %copy-start.41 = (f32[512]{0:T(512)S(1)}, f32[512]{0:T(512)}, u32[]{:S(2)}) copy-start(f32[512]{0:T(512)} %copy-done.40) | copy-start | bytes 6148
  635.6 88.5 %copy-start.10 = (f32[512,1024]{1,0:T(8,128)S(1)}, f32[512,1024]{1,0:T(8,128)}, u32[]{:S(2)}) copy-start(f32[512,1024]{1,0:T(8,128)} %copy-done.9) | copy-start | bytes 6291460
  854.6 11.4 %copy-start.1 = (bf16[1024,1024]{1,0:T(8,128)(2,1)S(1)}, bf16[1024,1024]{1,0:T(8,128)(2,1)}, u32[]{:S(2)}) copy-start(bf16[1024,1024]{1,0:T(8,128)(2,1)} %param.21) | copy-start | bytes 6291460
  (16 other events, 25.5 us)
Sparse Core Ops, SparseCore 0:
  15.5 37.1 all-gather.6
  110.2 44.5 reduce-scatter.4
  160.1 34.4 all-gather.8
  196.0 34.4 all-gather.10
  266.2 44.5 reduce-scatter.8
  313.2 44.5 reduce-scatter.6
  364.3 34.4 all-gather.12
  459.1 170.1 all-reduce.6
  631.8 43.5 reduce-scatter.10
  677.5 177.0 all-gather.14
